TPU v7x, 512 devices: a whole 4x4x16 slice. The times are simulated.
512 devices in a mesh: layer: 2 (over y_lo), feat: 64 (over y_hi, z, core), width: 4 (over x).
Axes of the slice: x: 4, y: 4 (y_hi: 2, y_lo: 2; y = y_hi * 2 + y_lo), z: 16, core: 2. Of those that a mesh axis runs over, the one named last changes fastest.
Arguments:
- inputs: float32 [2, 1024, 2048], P('layer', None, 'width'), may hold values from -6 to 6
- targets: float32 [2, 1024, 2048], P(None, ('layer', 'feat'), 'width'), may hold values from -6 to 6
- w_enc: float32 [2, 2048, 16384], P('layer', 'width', 'feat'), may hold values from -0.125 to 0.125
- b_enc: float32 [2, 16384], P('layer', 'feat'), may hold values from -3 to 3
- thresholds: float32 [2, 16384], P('layer', 'feat'), may hold values from 0.2 to 1
- w_dec: float32 [2, 2, 16384, 2048], P('layer', None, 'feat', 'width'), may hold values from -0.046875 to 0.046875
- b_dec: float32 [2, 2048], P(None, 'width'), may hold values from -3 to 3
Outputs:
- dec_grad: float32 [2, 2, 16384, 2048], P('layer', None, 'feat', 'width')
- pre_grad: float32 [2, 1024, 16384], P('layer', 'width', 'feat')
All inputs are finite; a program needn't handle non-finite values.
Results may differ from a plain program's by a relative error of at most 0.0001.
Values sent between devices are 32-bit elements; how exact they have to be, the bound alone decides.
A program may use at most 64 MiB of HBM per device.

v0:
```python
import jax
import jax.numpy as jnp
from jax import lax
from jax.sharding import PartitionSpec as P

softness = 0.5


def local(inputs, targets, w_enc, b_enc, thresholds, w_dec, b_dec):
    highest = lax.Precision.HIGHEST
    layer_pos = lax.axis_index("layer")
    layer_total = w_dec.shape[1]
    row_count = inputs.shape[1]
    partial_value = jnp.dot(
        inputs[0], w_enc[0], precision=highest, preferred_element_type=jnp.float32
    )
    pre_act = lax.psum(partial_value, "width") + b_enc[0][None, :]
    gate_open = jax.nn.sigmoid((pre_act - thresholds[0][None, :]) / softness)
    activations = pre_act * gate_open
    slope_val = gate_open + pre_act * gate_open * (1.0 - gate_open) / softness
    partials = []
    for target_pos in range(layer_total):
        product = jnp.dot(
            activations, w_dec[0, target_pos], precision=highest, preferred_element_type=jnp.float32
        )
        partials.append(jnp.where(target_pos >= layer_pos, product, 0.0))
    stacked = jnp.stack(partials)
    share_rows = targets.shape[1]
    row_start = lax.axis_index(("layer", "feat")) * share_rows
    own_rows = lax.dynamic_slice_in_dim(stacked, row_start, share_rows, 1) - targets
    stacked = lax.dynamic_update_slice(stacked, own_rows, (jnp.int32(0), row_start, jnp.int32(0)))
    errors = lax.psum(stacked, ("layer", "feat")) + b_dec[:, None, :]
    dec_grads = []
    for target_pos in range(layer_total):
        product = lax.dot_general(
            activations,
            errors[target_pos],
            (((0,), (0,)), ((), ())),
            precision=highest,
            preferred_element_type=jnp.float32,
        )
        dec_grads.append(jnp.where(target_pos >= layer_pos, product, 0.0))
    dec_grad = jnp.stack(dec_grads)[None]
    width_rows = row_count // lax.axis_size("width")
    back_sum = jnp.zeros((lax.axis_size("width") * width_rows, w_dec.shape[2]), jnp.float32)
    for target_pos in range(layer_total):
        product = lax.dot_general(
            errors[target_pos],
            w_dec[0, target_pos],
            (((1,), (1,)), ((), ())),
            precision=highest,
            preferred_element_type=jnp.float32,
        )
        back_sum = back_sum + jnp.where(target_pos >= layer_pos, product, 0.0)
    back_rows = lax.psum_scatter(back_sum, "width", scatter_dimension=0, tiled=True)
    slope_rows = lax.dynamic_slice_in_dim(
        slope_val, lax.axis_index("width") * width_rows, width_rows, 0
    )
    pre_grad = (back_rows * slope_rows)[None]
    return (dec_grad, pre_grad)


def solution(mesh):
    in_specs = (
        P("layer", None, "width"),
        P(None, ("layer", "feat"), "width"),
        P("layer", "width", "feat"),
        P("layer", "feat"),
        P("layer", "feat"),
        P("layer", None, "feat", "width"),
        P(None, "width"),
    )
    out_specs = (P("layer", None, "feat", "width"), P("layer", "width", "feat"))
    return jax.shard_map(local, mesh=mesh, in_specs=in_specs, out_specs=out_specs, check_vma=False)
```

profile of v0, /device:TPU:1, one launch (start us, length us, event | category | flops | bytes accessed | tf_op | source)
XLA Modules:
  0.0 497.1 jit_solution(11323719065684853259)
XLA Ops:
  7.2 0.0 copy-start
  7.2 0.0 copy-start.6
  7.2 0.0 copy-start.7
  7.2 0.0 all-reduce.3.cloned.1.call-start
  7.2 1.5 copy-done
  8.8 3.8 fusion
  12.6 0.0 all-reduce.3.cloned.1.call-update
  12.6 0.0 all-reduce.5.cloned.1.call-start
  12.7 64.9 %all-reduce.3.cloned.1.call-done = f32[1024,256]{1,0:T(8,128)} async-done(((f32[1024,256]{1,0:T(8,128)}), f32[1024,256]{1,0:T(8,128)}) %all-reduce.3.cloned.1.call-update) | async-done | bytes 1048592 | tf_op jit(solution)/shard_map/psum | solution.py:17
  77.6 0.0 copy-done.6
  77.6 0.0 copy-done.7
  77.6 2.6 add_divide_fusion
  80.2 2.9 select_bitcast_fusion
  83.1 0.0 copy-done.2
  83.1 1.8 select_bitcast_fusion.1
  84.9 0.0 copy-start.4
  84.9 2.4 pad_maximum_fusion
  87.4 0.0 copy-done.4
  87.4 0.6 subtract_dynamic-update-slice_fusion
  88.0 0.0 all-reduce.5.cloned.1.call-update
  88.0 0.2 reduce-scatter.2.cloned.1.call-start
  88.2 362.9 %all-reduce.5.cloned.1.call-done = f32[2,1024,512]{2,1,0:T(8,128)} async-done(((f32[2,1024,512]{2,1,0:T(8,128)}), f32[2,1024,512]{2,1,0:T(8,128)}) %all-reduce.5.cloned.1.call-update) | async-done | bytes 4194320 | tf_op jit(solution)/shard_map/psum | solution.py:32
  451.2 2.8 broadcast_add_fusion
  454.0 1.8 fusion.8
  455.9 0.1 copy-done.1
  456.0 2.8 fusion.7
  458.8 0.0 reduce-scatter.2.cloned.1.call-update
  458.8 3.5 fusion.10
  462.4 3.5 fusion.12
  465.9 1.0 maximum_bitcast_fusion
  467.0 21.8 %reduce-scatter.2.cloned.1.call-done = f32[256,256]{1,0:T(8,128)} async-done(((f32[1024,256]{1,0:T(8,128)}), f32[256,256]{1,0:T(8,128)}) %reduce-scatter.2.cloned.1.call-update) | async-done | bytes 262160 | tf_op jit(solution)/shard_map/reduce_scatter | solution.py:55
  488.8 1.8 fusion.25
  (6 shorter events, 0.0 us)
Async XLA Ops:
  7.2 1.6 copy-start
  7.2 70.4 %copy-start.6 = (f32[1,256]{1,0:T(1,128)S(1)}, f32[1,256]{1,0:T(1,128)}, u32[]{:S(2)}) copy-start(f32[1,256]{1,0:T(1,128)} %param.11) | copy-start | bytes 3076
  7.2 70.4 %copy-start.7 = (f32[1,256]{1,0:T(1,128)S(1)}, f32[1,256]{1,0:T(1,128)}, u32[]{:S(2)}) copy-start(f32[1,256]{1,0:T(1,128)} %param.10) | copy-start | bytes 3076
  7.2 70.4 %all-reduce.3.cloned.1.call-start = ((), (), s32[]{:S(2)}) async-start(), calls=%async_computation.1 | async-start | bytes 2097152 | tf_op jit(solution)/shard_map/psum | solution.py:17
  12.6 438.6 %all-reduce.5.cloned.1.call-start = ((), (), s32[]{:S(2)}) async-start(), calls=%async_computation.2 | async-start | bytes 8388608 | tf_op jit(solution)/shard_map/psum | solution.py:32
  80.1 3.0 copy-start.2
  84.9 2.4 copy-start.4
  88.0 363.2 %copy-start.5 = (f32[2,512]{1,0:T(2,128)S(1)}, f32[2,512]{1,0:T(2,128)}, u32[]{:S(2)}) copy-start(f32[2,512]{1,0:T(2,128)} %param.13) | copy-start | bytes 12292
  88.0 400.8 %reduce-scatter.2.cloned.1.call-start = ((), (), s32[]{:S(2)}) async-start(), calls=%async_computation.3 | async-start | bytes 1310720 | tf_op jit(solution)/shard_map/reduce_scatter | solution.py:55
  451.2 2.9 copy-start.3
  454.0 1.9 copy-start.1
Sparse Core Ops, SparseCore 0:
  12.7 64.8 all-reduce.2
  88.1 362.9 all-reduce.4
  459.0 29.7 reduce-scatter.1
where the time goes:
time: 498 us; the launch traced here: 497 us
  waiting for transfers between devices  450 us (90%)
  matrix products  20.3 us (4%)
  between operations  13.9 us (3%)
  other arithmetic  11.3 us (2%)
    psum x1, waiting for transfers between devices, local(): errors = lax.psum(stacked, ('layer', 'feat')) + b_dec[:, None, :]  363 us
    psum x1, waiting for transfers between devices, local(): pre_act = lax.psum(partial_value, 'width') + b_enc[0][None, :]  64.9 us
    reduce_scatter x1, waiting for transfers between devices, local(): lax.psum_scatter(back_sum, 'width', scatter_dimension=0, tiled=True)  21.8 us
  transfers between devices with their start and end apart: 3, of which 3 were waited for; matrix products, arithmetic and copies ran while one was open for 2% of the time, Pallas kernels for 0%

commit v1 on v0

v1 whole, which is shorter than its diff:
```python
import functools

import jax
import jax.numpy as jnp
from jax import lax
from jax.experimental import pallas as pl
from jax.experimental.pallas import tpu as pltpu
from jax.sharding import PartitionSpec as P

softness = 0.5
MESH = pl.DeviceIdType.MESH
CHUNKS = 4
NX = 4
NY = 4
NZ = 16
F32 = jnp.float32
BF16 = jnp.bfloat16

STAGES = (
    ("pre", 1.5),
    ("gate", 5.5),
    ("recon", 5.5),
    ("core_sum", 2.5),
    ("y_sum", 7.5),
    ("zlo_sum", 6.0),
    ("zhi_sum", 8.0),
    ("zhi_all", 8.0),
    ("zlo_all", 6.0),
    ("y_all", 7.5),
    ("back", 2.5),
    ("grad", 0.3),
    ("finish", 5.5),
)


def stage_order(chunks):
    ready = []
    for chunk in range(chunks):
        when = chunk * 4.0
        for place, (name, wait) in enumerate(STAGES):
            when += wait
            ready.append((when, place, chunk, name))
    return [(name, chunk) for _, _, chunk, name in sorted(ready)]


def split(value):
    high = value.astype(BF16)
    low = (value - high.astype(F32)).astype(BF16)
    return high, low


def product(a, b, dims):
    dot = functools.partial(
        lax.dot_general, dimension_numbers=(dims, ((), ())), preferred_element_type=F32
    )
    return dot(a[0], b[0]) + (dot(a[0], b[1]) + dot(a[1], b[0]))


NN = ((1,), (0,))
NT = ((1,), (1,))


def kernel(
    x_hbm,
    targets_ref,
    enc_hbm,
    b_enc_ref,
    thr_ref,
    dec_hbm,
    b_dec_ref,
    dec_grad_ref,
    pre_grad_ref,
    x_ref,
    enc_f32,
    dec_f32,
    enc,
    dec,
    pre_part,
    pre_recv,
    acts,
    slope,
    q_send,
    q_own,
    q_recv,
    y_recv,
    zlo_part,
    zlo_recv,
    zhi_part,
    zhi_recv,
    errs,
    back_part,
    back_recv,
    load_sem,
    x_ss,
    x_rs,
    y_ss,
    y_rs,
    zlo_ss,
    zlo_rs,
    zhi_ss,
    zhi_rs,
    c_ss,
    c_rs,
):
    layer = lax.axis_index("layer")
    feat = lax.axis_index("feat")
    width = lax.axis_index("width")
    core = lax.rem(feat, 2)
    z = lax.rem(feat // 2, NZ)
    zlo = lax.rem(z, 4)
    zhi = z // 4
    y = (feat // (2 * NZ)) * 2 + layer
    chunks, _, rows, _ = acts.shape
    block = 2 * rows // NZ

    def turn(place, step):
        return lax.rem(place + step, 4)

    def device(y_at, z_at, core_at, x_at):
        return (lax.rem(y_at, 2), (y_at // 2) * (2 * NZ) + z_at * 2 + core_at, x_at)

    def x_peer(step):
        return device(y, z, core, turn(width, step))

    def y_peer(step):
        return device(turn(y, step), z, core, width)

    def zlo_peer(step):
        return device(y, zhi * 4 + turn(zlo, step), core, width)

    def zhi_peer(step):
        return device(y, turn(zhi, step) * 4 + zlo, core, width)

    partner = device(y, z, 1 - core, width)
    peers = [partner] + [peer(step) for peer in (x_peer, y_peer, zlo_peer, zhi_peer) for step in (1, 2, 3)]

    loads = [
        pltpu.make_async_copy(enc_hbm, enc_f32, load_sem.at[0]),
        pltpu.make_async_copy(x_hbm, x_ref, load_sem.at[1]),
        pltpu.make_async_copy(dec_hbm, dec_f32, load_sem.at[2]),
    ]
    for load in loads:
        load.start()
    barrier = pltpu.get_barrier_semaphore()
    for peer in peers:
        pl.semaphore_signal(barrier, inc=1, device_id=peer, device_id_type=MESH)

    sent = []

    def send(src, dst, send_sem, recv_sem, peer):
        copy = pltpu.make_async_remote_copy(
            src_ref=src,
            dst_ref=dst,
            send_sem=send_sem,
            recv_sem=recv_sem,
            device_id=peer,
            device_id_type=MESH,
        )
        copy.start()
        sent.append(copy)
        return copy

    pending = {}

    def arrive(key):
        for copy in pending.pop(key):
            copy.wait_recv()

    loads[0].wait()
    high, low = split(enc_f32[...])
    enc[0] = high
    enc[1] = low
    loads[1].wait()
    pl.semaphore_wait(barrier, len(peers))

    def load_dec():
        loads[2].wait()
        for target in range(2):
            for half in range(2):
                value = dec_f32[target, :, half * 256 : (half + 1) * 256]
                if target == 0:
                    value = jnp.where(layer == 0, value, 0.0)
                high, low = split(value)
                dec[half, target, 0] = high
                dec[half, target, 1] = low

    def pre(c):
        value = x_ref[:, c].reshape(4 * rows, x_ref.shape[3])
        part = product(split(value), (enc[0], enc[1]), NN)
        pre_part[c] = part.reshape(4, rows, 256)
        pending["pre", c] = [
            send(
                pre_part.at[c, turn(width, step)],
                pre_recv.at[c, step - 1],
                x_ss.at[0, c, step - 1],
                x_rs.at[0, c, step - 1],
                x_peer(step),
            )
            for step in (1, 3, 2)
        ]
        if c == 0:
            load_dec()

    def gate(c):
        arrive(("pre", c))
        total = pre_part[c, width] + pre_recv[c, 0] + pre_recv[c, 1] + pre_recv[c, 2]
        total = total + b_enc_ref[...]
        opened = jax.nn.sigmoid((total - thr_ref[...]) / softness)
        acts[c, width] = total * opened
        slope[c] = opened + total * opened * (1.0 - opened) / softness
        pending["acts", c] = [
            send(
                acts.at[c, width],
                acts.at[c, width],
                x_ss.at[1, c, step - 1],
                x_rs.at[1, c, step - 1],
                x_peer(step),
            )
            for step in (1, 3, 2)
        ]

    first = (layer * 64 + feat) * targets_ref.shape[1]
    own_x = first // (rows * chunks)
    own_chunk = lax.rem(first, rows * chunks) // rows
    own_row = pl.multiple_of(lax.rem(first, rows), 8)

    def recon(c):
        arrive(("acts", c))
        value = split(acts[c].reshape(4 * rows, 256))
        for dst, half in ((q_send, 1 - core), (q_own, core)):
            for target in range(2):
                part = product(value, (dec[half, target, 0], dec[half, target, 1]), NN)
                dst[c, :, target * rows : (target + 1) * rows, :] = part.reshape(4, rows, 256)

            @pl.when(own_chunk == c)
            def _():
                for target in range(2):
                    at = pl.multiple_of(target * rows + own_row, 8)
                    spot = (c, own_x, pl.ds(at, 8), slice(None))
                    columns = pl.ds(pl.multiple_of(half * 256, 256), 256)
                    dst[spot] = dst[spot] - targets_ref[target, :, columns]

            if dst is q_send:
                pending["q", c] = [
                    send(q_send.at[c], q_recv.at[c], c_ss.at[0, c], c_rs.at[0, c], partner)
                ]

    def core_sum(c):
        arrive(("q", c))
        copies = []
        for step in (1, 3, 2):
            at = turn(y, step)
            q_own[c, at] = q_own[c, at] + q_recv[c, at]
            copies.append(
                send(
                    q_own.at[c, at],
                    y_recv.at[c, step - 1],
                    y_ss.at[0, c, step - 1],
                    y_rs.at[0, c, step - 1],
                    y_peer(step),
                )
            )
        pending["y", c] = copies

    def y_sum(c):
        arrive(("y", c))
        total = (q_own[c, y] + q_recv[c, y]) + (y_recv[c, 0] + y_recv[c, 1] + y_recv[c, 2])
        zlo_part[c] = total.reshape(4, 4 * block, 256)
        pending["zlo", c] = [
            send(
                zlo_part.at[c, turn(zlo, step)],
                zlo_recv.at[c, step - 1],
                zlo_ss.at[0, c, step - 1],
                zlo_rs.at[0, c, step - 1],
                zlo_peer(step),
            )
            for step in (1, 3, 2)
        ]

    def zlo_sum(c):
        arrive(("zlo", c))
        total = zlo_part[c, zlo] + (zlo_recv[c, 0] + zlo_recv[c, 1] + zlo_recv[c, 2])
        zhi_part[c] = total.reshape(4, block, 256)
        pending["zhi", c] = [
            send(
                zhi_part.at[c, turn(zhi, step)],
                zhi_recv.at[c, step - 1],
                zhi_ss.at[0, c, step - 1],
                zhi_rs.at[0, c, step - 1],
                zhi_peer(step),
            )
            for step in (2, 1, 3)
        ]

    def zhi_sum(c):
        arrive(("zhi", c))
        total = zhi_part[c, zhi] + (zhi_recv[c, 0] + zhi_recv[c, 1] + zhi_recv[c, 2])
        columns = pl.ds(pl.multiple_of(core * 256, 256), 256)
        bias = b_dec_ref[:, columns]
        total = total + jnp.where(zlo >= 2, bias[1:2], bias[0:1])
        errs[c, core, y, zlo, zhi] = total
        own = errs.at[c, core, y, zlo, zhi]
        pending["zhi_all", c] = [
            send(own, own, zhi_ss.at[1, c, step - 1], zhi_rs.at[1, c, step - 1], zhi_peer(step))
            for step in (2, 1, 3)
        ]

    def zhi_all(c):
        arrive(("zhi_all", c))
        own = errs.at[c, core, y, zlo]
        pending["zlo_all", c] = [
            send(own, own, zlo_ss.at[1, c, step - 1], zlo_rs.at[1, c, step - 1], zlo_peer(step))
            for step in (1, 3, 2)
        ]

    def zlo_all(c):
        arrive(("zlo_all", c))
        own = errs.at[c, core, y]
        pending["y_all", c] = [
            send(own, own, y_ss.at[1, c, step - 1], y_rs.at[1, c, step - 1], y_peer(step))
            for step in (1, 3, 2)
        ]

    def y_all(c):
        arrive(("y_all", c))
        own = errs.at[c, core]
        pending["e", c] = [send(own, own, c_ss.at[1, c], c_rs.at[1, c], partner)]

    def error_of(c, half, target):
        value = errs[c, half].reshape(4, 2 * rows, 256)
        return value[:, target * rows : (target + 1) * rows].reshape(4 * rows, 256)

    def back(c):
        arrive(("e", c))
        total = None
        for half in range(2):
            for target in range(2):
                value = split(error_of(c, half, target))
                part = product(value, (dec[half, target, 0], dec[half, target, 1]), NT)
                total = part if total is None else total + part
        back_part[c] = total.reshape(4, rows, 256)
        pending["back", c] = [
            send(
                back_part.at[c, turn(width, step)],
                back_recv.at[c, step - 1],
                x_ss.at[2, c, step - 1],
                x_rs.at[2, c, step - 1],
                x_peer(step),
            )
            for step in (1, 3, 2)
        ]

    def grad(c):
        turned = split(acts[c].reshape(4 * rows, 256).T)
        for target in range(2):
            for half in range(2):
                part = product(turned, split(error_of(c, half, target)), NN)
                if target == 0:
                    part = jnp.where(layer == 0, part, 0.0)
                columns = slice(half * 256, (half + 1) * 256)
                if c == 0:
                    dec_grad_ref[target, :, columns] = part
                else:
                    dec_grad_ref[target, :, columns] += part

    def finish(c):
        arrive(("back", c))
        total = back_part[c, width] + (back_recv[c, 0] + back_recv[c, 1] + back_recv[c, 2])
        pre_grad_ref[c * rows : (c + 1) * rows, :] = total * slope[c]

    run = locals()
    stages = {name: run[name] for name, _ in STAGES}
    for name, c in stage_order(chunks):
        stages[name](c)
    for copy in sent:
        copy.wait_send()


def local(inputs, targets, w_enc, b_enc, thresholds, w_dec, b_dec):
    tokens, width = inputs.shape[1:]
    feats = w_enc.shape[2]
    c = CHUNKS
    rows = tokens // (NX * c)
    block = 2 * rows // NZ
    half = width // 2
    vmem = pl.BlockSpec(memory_space=pltpu.VMEM)
    anywhere = pl.BlockSpec(memory_space=pl.ANY)
    dma = pltpu.SemaphoreType.DMA
    dec_grad, pre_grad = pl.pallas_call(
        kernel,
        out_shape=(
            jax.ShapeDtypeStruct(w_dec.shape[1:], F32),
            jax.ShapeDtypeStruct((tokens // NX, feats), F32),
        ),
        in_specs=[anywhere, vmem, anywhere, vmem, vmem, anywhere, vmem],
        out_specs=(vmem, vmem),
        scratch_shapes=[
            pltpu.VMEM((NX, c, rows, width), F32),
            pltpu.VMEM((width, feats), F32),
            pltpu.VMEM((2, feats, width), F32),
            pltpu.VMEM((2, width, feats), BF16),
            pltpu.VMEM((2, 2, 2, feats, half), BF16),
            pltpu.VMEM((c, NX, rows, feats), F32),
            pltpu.VMEM((c, 3, rows, feats), F32),
            pltpu.VMEM((c, NX, rows, feats), F32),
            pltpu.VMEM((c, rows, feats), F32),
            pltpu.VMEM((c, NY, 2 * rows, half), F32),
            pltpu.VMEM((c, NY, 2 * rows, half), F32),
            pltpu.VMEM((c, NY, 2 * rows, half), F32),
            pltpu.VMEM((c, 3, 2 * rows, half), F32),
            pltpu.VMEM((c, 4, 4 * block, half), F32),
            pltpu.VMEM((c, 3, 4 * block, half), F32),
            pltpu.VMEM((c, 4, block, half), F32),
            pltpu.VMEM((c, 3, block, half), F32),
            pltpu.VMEM((c, 2, NY, 4, 4, block, half), F32),
            pltpu.VMEM((c, NX, rows, feats), F32),
            pltpu.VMEM((c, 3, rows, feats), F32),
            dma((3,)),
            dma((3, c, 3)),
            dma((3, c, 3)),
            dma((2, c, 3)),
            dma((2, c, 3)),
            dma((2, c, 3)),
            dma((2, c, 3)),
            dma((2, c, 3)),
            dma((2, c, 3)),
            dma((2, c)),
            dma((2, c)),
        ],
        compiler_params=pltpu.CompilerParams(
            collective_id=0, has_side_effects=True, vmem_limit_bytes=60 * 1024 * 1024
        ),
    )(
        inputs.reshape(NX, c, rows, width),
        targets,
        w_enc[0],
        b_enc,
        thresholds,
        w_dec[0],
        b_dec,
    )
    return dec_grad[None], pre_grad[None]


def solution(mesh):
    in_specs = (
        P("layer", None, "width"),
        P(None, ("layer", "feat"), "width"),
        P("layer", "width", "feat"),
        P("layer", "feat"),
        P("layer", "feat"),
        P("layer", None, "feat", "width"),
        P(None, "width"),
    )
    out_specs = (P("layer", None, "feat", "width"), P("layer", "width", "feat"))
    return jax.shard_map(local, mesh=mesh, in_specs=in_specs, out_specs=out_specs, check_vma=False)
```

time: 498 us -> 117 us (0.23)
  waiting for transfers between devices: 450 us -> 0 us
  Pallas kernels: 0 us -> 114 us
  matrix products: 20.3 us -> 0 us
  between operations: 13.9 us -> 0.65 us
  other arithmetic: 11.3 us -> 0 us
    psum x2 -> x0, waiting for transfers between devices: 428 us -> none  [the longest x1 363 us: local(): errors = lax.psum(stacked, ('layer', 'feat')) + b_dec[:, None, :]]
    pallas_call x0 -> x1, Pallas kernels: none -> 114 us  [local(): pl.pallas_call(kernel, out_shape=(jax.ShapeDtypeStruct(w_dec.shape[1:], F...]
    reduce_scatter x1 -> x0, waiting for transfers between devices: 21.8 us -> none  [local(): lax.psum_scatter(back_sum, 'width', scatter_dimension=0, tiled=True)]
    dot_general x7 -> x0, matrix products: 20.3 us -> none  [the longest x2 7.07 us: local(): lax.dot_general(activations, errors[target_pos], (((0,), (0,)), ((), ()))...]
  transfers between devices with their start and end apart: 3 -> 0, of which waited for: 3 -> 0; matrix products, arithmetic and copies ran while one was open for 2% -> 0% of each run, Pallas kernels for 0% -> 0%
where the time goes in v1:
time: 117 us
  Pallas kernels  114 us (97%)
  local copies, waits for them, and re-layouts  3.01 us (3%)
    pallas_call x1, Pallas kernels, local(): pl.pallas_call(kernel, out_shape=(jax.ShapeDtypeStruct(w_dec.shape[1:], F...  114 us
    unnamed x4, local copies, waits for them, and re-layouts  3.01 us

profile of v1, /device:TPU:1, one launch (start us, length us, event | category | flops | bytes accessed | tf_op | source)
XLA Modules:
  0.0 117.3 jit_solution(17505104808479020552)
XLA Ops:
  0.6 113.6 %shard_map.86 = (f32[2,256,512]{2,1,0:T(8,128)}, f32[256,256]{1,0:T(8,128)}) custom-call(f32[4,4,64,512]{3,2,1,0:T(8,128)} %bitcast.5, f32[2,8,512]{2,1,0:T(8,128)} %targets_ref.1, f32[512,256]{1,0:T(8,128)} %bitcast.8, f32[1,256]{1,0:T(1,128)} %b_enc_ref.1, f32[1,256]{1,0:T(1,128)} %thr_ref.1, f32[2,256,512]{2,1,0:T(8,128)} %bitcast.7, f32[2,512]{1,0:T(2,128)} %b_dec_ref.1), custom_call_target="tpu_custom_call" | custom-call | tf_op jit(solution)/shard_map/pallas_call | solution.py:389
  114.2 0.0 copy-start
  114.3 2.3 %copy.11 = f32[1,2,256,512]{3,2,1,0:T(8,128)} copy(f32[1,2,256,512]{3,2,1,0:T(8,128)} %bitcast.6) | data formatting | bytes 2097152
  116.6 0.0 copy-done
  116.6 0.7 copy.12
Async XLA Ops:
  114.2 2.3 %copy-start = (f32[256,256]{1,0:T(8,128)S(1)}, f32[256,256]{1,0:T(8,128)}, u32[]{:S(2)}) copy-start(f32[256,256]{1,0:T(8,128)} %get-tuple-element.5) | copy-start | bytes 786436

commit v2 on v1

--- a/solution.py
+++ b/solution.py
@@ -9,7 +9,8 @@
 
 softness = 0.5
 MESH = pl.DeviceIdType.MESH
-CHUNKS = 4
+CHUNKS = 8
+SPACING = 3.5
 NX = 4
 NY = 4
 NZ = 16
@@ -18,25 +19,25 @@
 
 STAGES = (
     ("pre", 1.5),
-    ("gate", 5.5),
-    ("recon", 5.5),
-    ("core_sum", 2.5),
-    ("y_sum", 7.5),
-    ("zlo_sum", 6.0),
-    ("zhi_sum", 8.0),
-    ("zhi_all", 8.0),
-    ("zlo_all", 6.0),
-    ("y_all", 7.5),
-    ("back", 2.5),
+    ("gate", 4.5),
+    ("recon", 4.5),
+    ("core_sum", 1.8),
+    ("y_sum", 5.3),
+    ("zlo_sum", 5.1),
+    ("zhi_sum", 7.5),
+    ("zhi_all", 7.5),
+    ("zlo_all", 5.1),
+    ("y_all", 5.3),
+    ("back", 1.8),
     ("grad", 0.3),
-    ("finish", 5.5),
+    ("finish", 4.5),
 )
 
 
 def stage_order(chunks):
     ready = []
     for chunk in range(chunks):
-        when = chunk * 4.0
+        when = chunk * SPACING
         for place, (name, wait) in enumerate(STAGES):
             when += wait
             ready.append((when, place, chunk, name))
@@ -62,14 +63,18 @@
 
 def kernel(
     x_hbm,
+    targets_hbm,
+    enc_hbm,
+    b_enc_hbm,
+    thr_hbm,
+    dec_hbm,
+    b_dec_hbm,
+    dec_grad_ref,
+    pre_grad_ref,
     targets_ref,
-    enc_hbm,
     b_enc_ref,
     thr_ref,
-    dec_hbm,
     b_dec_ref,
-    dec_grad_ref,
-    pre_grad_ref,
     x_ref,
     enc_f32,
     dec_f32,
@@ -111,7 +116,6 @@
     zhi = z // 4
     y = (feat // (2 * NZ)) * 2 + layer
     chunks, _, rows, _ = acts.shape
-    block = 2 * rows // NZ
 
     def turn(place, step):
         return lax.rem(place + step, 4)
@@ -136,10 +140,16 @@
 
     loads = [
         pltpu.make_async_copy(enc_hbm, enc_f32, load_sem.at[0]),
-        pltpu.make_async_copy(x_hbm, x_ref, load_sem.at[1]),
-        pltpu.make_async_copy(dec_hbm, dec_f32, load_sem.at[2]),
+        pltpu.make_async_copy(dec_hbm, dec_f32, load_sem.at[1]),
     ]
-    for load in loads:
+    x_loads = [
+        pltpu.make_async_copy(x_hbm.at[:, c], x_ref.at[:, c], load_sem.at[2 + c]) for c in range(chunks)
+    ]
+    small = ((b_enc_hbm, b_enc_ref), (thr_hbm, thr_ref), (targets_hbm, targets_ref), (b_dec_hbm, b_dec_ref))
+    small_loads = [
+        pltpu.make_async_copy(src, dst, load_sem.at[2 + chunks + place]) for place, (src, dst) in enumerate(small)
+    ]
+    for load in [loads[0], x_loads[0], *small_loads, loads[1], *x_loads[1:]]:
         load.start()
     barrier = pltpu.get_barrier_semaphore()
     for peer in peers:
@@ -170,11 +180,8 @@
     high, low = split(enc_f32[...])
     enc[0] = high
     enc[1] = low
-    loads[1].wait()
-    pl.semaphore_wait(barrier, len(peers))
 
     def load_dec():
-        loads[2].wait()
         for target in range(2):
             for half in range(2):
                 value = dec_f32[target, :, half * 256 : (half + 1) * 256]
@@ -185,9 +192,12 @@
                 dec[half, target, 1] = low
 
     def pre(c):
+        x_loads[c].wait()
         value = x_ref[:, c].reshape(4 * rows, x_ref.shape[3])
         part = product(split(value), (enc[0], enc[1]), NN)
         pre_part[c] = part.reshape(4, rows, 256)
+        if c == 0:
+            pl.semaphore_wait(barrier, len(peers))
         pending["pre", c] = [
             send(
                 pre_part.at[c, turn(width, step)],
@@ -199,6 +209,9 @@
             for step in (1, 3, 2)
         ]
         if c == 0:
+            loads[1].wait()
+            for load in small_loads:
+                load.wait()
             load_dec()
 
     def gate(c):
@@ -242,7 +255,7 @@
 
             if dst is q_send:
                 pending["q", c] = [
-                    send(q_send.at[c], q_recv.at[c], c_ss.at[0, c], c_rs.at[0, c], partner)
+                    send(q_send.at[c], q_recv.at[c], c_ss.at[0, c, 0], c_rs.at[0, c, 0], partner)
                 ]
 
     def core_sum(c):
@@ -265,7 +278,7 @@
     def y_sum(c):
         arrive(("y", c))
         total = (q_own[c, y] + q_recv[c, y]) + (y_recv[c, 0] + y_recv[c, 1] + y_recv[c, 2])
-        zlo_part[c] = total.reshape(4, 4 * block, 256)
+        zlo_part[c] = total.reshape(4, 2 * rows // 4, 256)
         pending["zlo", c] = [
             send(
                 zlo_part.at[c, turn(zlo, step)],
@@ -280,7 +293,9 @@
     def zlo_sum(c):
         arrive(("zlo", c))
         total = zlo_part[c, zlo] + (zlo_recv[c, 0] + zlo_recv[c, 1] + zlo_recv[c, 2])
-        zhi_part[c] = total.reshape(4, block, 256)
+        for part in range(4):
+            down, across = (part // 2) * 8, (part % 2) * 128
+            zhi_part[c, part] = total[down : down + 8, across : across + 128]
         pending["zhi", c] = [
             send(
                 zhi_part.at[c, turn(zhi, step)],
@@ -295,7 +310,7 @@
     def zhi_sum(c):
         arrive(("zhi", c))
         total = zhi_part[c, zhi] + (zhi_recv[c, 0] + zhi_recv[c, 1] + zhi_recv[c, 2])
-        columns = pl.ds(pl.multiple_of(core * 256, 256), 256)
+        columns = pl.ds(pl.multiple_of(core * 256 + lax.rem(zhi, 2) * 128, 128), 128)
         bias = b_dec_ref[:, columns]
         total = total + jnp.where(zlo >= 2, bias[1:2], bias[0:1])
         errs[c, core, y, zlo, zhi] = total
@@ -313,6 +328,10 @@
             for step in (1, 3, 2)
         ]
 
+    def pass_on(c, at):
+        own = errs.at[c, core, at]
+        return send(own, own, c_ss.at[1, c, at], c_rs.at[1, c, at], partner)
+
     def zlo_all(c):
         arrive(("zlo_all", c))
         own = errs.at[c, core, y]
@@ -320,15 +339,17 @@
             send(own, own, y_ss.at[1, c, step - 1], y_rs.at[1, c, step - 1], y_peer(step))
             for step in (1, 3, 2)
         ]
+        pending["e", c] = [pass_on(c, y)]
 
     def y_all(c):
-        arrive(("y_all", c))
-        own = errs.at[c, core]
-        pending["e", c] = [send(own, own, c_ss.at[1, c], c_rs.at[1, c], partner)]
+        for copy, step in zip(pending.pop(("y_all", c)), (1, 3, 2)):
+            copy.wait_recv()
+            pending["e", c].append(pass_on(c, turn(y, -step + 4)))
 
     def error_of(c, half, target):
-        value = errs[c, half].reshape(4, 2 * rows, 256)
-        return value[:, target * rows : (target + 1) * rows].reshape(4 * rows, 256)
+        value = errs[c, half, :, 2 * target : 2 * target + 2].reshape(4, 2, 2, 2, 8, 128)
+        sides = [value[:, :, :, side].reshape(4 * rows, 128) for side in range(2)]
+        return jnp.concatenate(sides, axis=1)
 
     def back(c):
         arrive(("e", c))
@@ -351,14 +372,17 @@
         ]
 
     def grad(c):
-        turned = split(acts[c].reshape(4 * rows, 256).T)
+        if c % 2 == 0:
+            return
+        turned = split(acts[c - 1 : c + 1].reshape(8 * rows, 256).T)
         for target in range(2):
             for half in range(2):
-                part = product(turned, split(error_of(c, half, target)), NN)
+                value = jnp.concatenate([error_of(c - 1, half, target), error_of(c, half, target)], axis=0)
+                part = product(turned, split(value), NN)
                 if target == 0:
                     part = jnp.where(layer == 0, part, 0.0)
                 columns = slice(half * 256, (half + 1) * 256)
-                if c == 0:
+                if c == 1:
                     dec_grad_ref[target, :, columns] = part
                 else:
                     dec_grad_ref[target, :, columns] += part
@@ -381,10 +405,9 @@
     feats = w_enc.shape[2]
     c = CHUNKS
     rows = tokens // (NX * c)
-    block = 2 * rows // NZ
     half = width // 2
     vmem = pl.BlockSpec(memory_space=pltpu.VMEM)
-    anywhere = pl.BlockSpec(memory_space=pl.ANY)
+    hbm = pl.BlockSpec(memory_space=pltpu.HBM)
     dma = pltpu.SemaphoreType.DMA
     dec_grad, pre_grad = pl.pallas_call(
         kernel,
@@ -392,9 +415,13 @@
             jax.ShapeDtypeStruct(w_dec.shape[1:], F32),
             jax.ShapeDtypeStruct((tokens // NX, feats), F32),
         ),
-        in_specs=[anywhere, vmem, anywhere, vmem, vmem, anywhere, vmem],
+        in_specs=[hbm] * 7,
         out_specs=(vmem, vmem),
         scratch_shapes=[
+            pltpu.VMEM(targets.shape, F32),
+            pltpu.VMEM((1, feats), F32),
+            pltpu.VMEM((1, feats), F32),
+            pltpu.VMEM(b_dec.shape, F32),
             pltpu.VMEM((NX, c, rows, width), F32),
             pltpu.VMEM((width, feats), F32),
             pltpu.VMEM((2, feats, width), F32),
@@ -408,14 +435,14 @@
             pltpu.VMEM((c, NY, 2 * rows, half), F32),
             pltpu.VMEM((c, NY, 2 * rows, half), F32),
             pltpu.VMEM((c, 3, 2 * rows, half), F32),
-            pltpu.VMEM((c, 4, 4 * block, half), F32),
-            pltpu.VMEM((c, 3, 4 * block, half), F32),
-            pltpu.VMEM((c, 4, block, half), F32),
-            pltpu.VMEM((c, 3, block, half), F32),
-            pltpu.VMEM((c, 2, NY, 4, 4, block, half), F32),
+            pltpu.VMEM((c, 4, 2 * rows // 4, half), F32),
+            pltpu.VMEM((c, 3, 2 * rows // 4, half), F32),
+            pltpu.VMEM((c, 4, 8, 128), F32),
+            pltpu.VMEM((c, 3, 8, 128), F32),
+            pltpu.VMEM((c, 2, NY, 4, 4, 8, 128), F32),
             pltpu.VMEM((c, NX, rows, feats), F32),
             pltpu.VMEM((c, 3, rows, feats), F32),
-            dma((3,)),
+            dma((6 + c,)),
             dma((3, c, 3)),
             dma((3, c, 3)),
             dma((2, c, 3)),
@@ -424,11 +451,11 @@
             dma((2, c, 3)),
             dma((2, c, 3)),
             dma((2, c, 3)),
-            dma((2, c)),
-            dma((2, c)),
+            dma((2, c, 4)),
+            dma((2, c, 4)),
         ],
         compiler_params=pltpu.CompilerParams(
-            collective_id=0, has_side_effects=True, vmem_limit_bytes=60 * 1024 * 1024
+            collective_id=0, has_side_effects=True, vmem_limit_bytes=54 * 1024 * 1024
         ),
     )(
         inputs.reshape(NX, c, rows, width),

time: 117 us -> 104 us (0.89)
  Pallas kernels: 114 us -> 100 us
    pallas_call x1, Pallas kernels: 114 us -> 100 us  [local(): pl.pallas_call(kernel, out_shape=(jax.ShapeDtypeStruct(w_dec.shape[1:], F...]
where the time goes in v2:
time: 104 us
  Pallas kernels  100 us (96%)
  local copies, waits for them, and re-layouts  3.01 us (3%)
    pallas_call x1, Pallas kernels, local(): pl.pallas_call(kernel, out_shape=(jax.ShapeDtypeStruct(w_dec.shape[1:], F...  100 us
    unnamed x4, local copies, waits for them, and re-layouts  3.01 us

profile of v2, /device:TPU:1, one launch (start us, length us, event | category | flops | bytes accessed | tf_op | source)
XLA Modules:
  0.0 103.8 jit_solution(18289565347442286436)
XLA Ops:
  0.6 100.1 %shard_map.86 = (f32[2,256,512]{2,1,0:T(8,128)}, f32[256,256]{1,0:T(8,128)}) custom-call(f32[4,8,32,512]{3,2,1,0:T(8,128)} %bitcast.5, f32[2,8,512]{2,1,0:T(8,128)} %targets_hbm.1, f32[512,256]{1,0:T(8,128)} %bitcast.8, f32[1,256]{1,0:T(1,128)} %b_enc_hbm.1, f32[1,256]{1,0:T(1,128)} %thr_hbm.1, f32[2,256,512]{2,1,0:T(8,128)} %bitcast.7, f32[2,512]{1,0:T(2,128)} %b_dec_hbm.1), custom_call_target="tpu_custom_call" | custom-call | tf_op jit(solution)/shard_map/pallas_call | solution.py:412
  100.8 0.0 copy-start
  100.8 2.3 %copy.11 = f32[1,2,256,512]{3,2,1,0:T(8,128)} copy(f32[1,2,256,512]{3,2,1,0:T(8,128)} %bitcast.6) | data formatting | bytes 2097152
  103.1 0.0 copy-done
  103.1 0.7 copy.12
Async XLA Ops:
  100.8 2.3 %copy-start = (f32[256,256]{1,0:T(8,128)S(1)}, f32[256,256]{1,0:T(8,128)}, u32[]{:S(2)}) copy-start(f32[256,256]{1,0:T(8,128)} %get-tuple-element.5) | copy-start | bytes 786436

commit v3 on v2

--- a/solution.py
+++ b/solution.py
@@ -19,8 +19,8 @@
 
 STAGES = (
     ("pre", 1.5),
-    ("gate", 4.5),
-    ("recon", 4.5),
+    ("gate", 6.0),
+    ("recon", 6.0),
     ("core_sum", 1.8),
     ("y_sum", 5.3),
     ("zlo_sum", 5.1),
@@ -30,7 +30,7 @@
     ("y_all", 5.3),
     ("back", 1.8),
     ("grad", 0.3),
-    ("finish", 4.5),
+    ("finish", 6.0),
 )
 
 
@@ -69,8 +69,11 @@
     thr_hbm,
     dec_hbm,
     b_dec_hbm,
+    dec_grad_hbm,
+    pre_grad_hbm,
     dec_grad_ref,
     pre_grad_ref,
+    out_sem,
     targets_ref,
     b_enc_ref,
     thr_ref,
@@ -156,6 +159,7 @@
         pl.semaphore_signal(barrier, inc=1, device_id=peer, device_id_type=MESH)
 
     sent = []
+    stored = []
 
     def send(src, dst, send_sem, recv_sem, peer):
         copy = pltpu.make_async_remote_copy(
@@ -206,7 +210,7 @@
                 x_rs.at[0, c, step - 1],
                 x_peer(step),
             )
-            for step in (1, 3, 2)
+            for step in (2, 1, 3)
         ]
         if c == 0:
             loads[1].wait()
@@ -229,7 +233,7 @@
                 x_rs.at[1, c, step - 1],
                 x_peer(step),
             )
-            for step in (1, 3, 2)
+            for step in (2, 1, 3)
         ]
 
     first = (layer * 64 + feat) * targets_ref.shape[1]
@@ -261,7 +265,7 @@
     def core_sum(c):
         arrive(("q", c))
         copies = []
-        for step in (1, 3, 2):
+        for step in (2, 1, 3):
             at = turn(y, step)
             q_own[c, at] = q_own[c, at] + q_recv[c, at]
             copies.append(
@@ -287,7 +291,7 @@
                 zlo_rs.at[0, c, step - 1],
                 zlo_peer(step),
             )
-            for step in (1, 3, 2)
+            for step in (2, 1, 3)
         ]
 
     def zlo_sum(c):
@@ -325,7 +329,7 @@
         own = errs.at[c, core, y, zlo]
         pending["zlo_all", c] = [
             send(own, own, zlo_ss.at[1, c, step - 1], zlo_rs.at[1, c, step - 1], zlo_peer(step))
-            for step in (1, 3, 2)
+            for step in (2, 1, 3)
         ]
 
     def pass_on(c, at):
@@ -337,12 +341,12 @@
         own = errs.at[c, core, y]
         pending["y_all", c] = [
             send(own, own, y_ss.at[1, c, step - 1], y_rs.at[1, c, step - 1], y_peer(step))
-            for step in (1, 3, 2)
+            for step in (2, 1, 3)
         ]
         pending["e", c] = [pass_on(c, y)]
 
     def y_all(c):
-        for copy, step in zip(pending.pop(("y_all", c)), (1, 3, 2)):
+        for copy, step in zip(pending.pop(("y_all", c)), (2, 1, 3)):
             copy.wait_recv()
             pending["e", c].append(pass_on(c, turn(y, -step + 4)))
 
@@ -368,7 +372,7 @@
                 x_rs.at[2, c, step - 1],
                 x_peer(step),
             )
-            for step in (1, 3, 2)
+            for step in (2, 1, 3)
         ]
 
     def grad(c):
@@ -386,11 +390,20 @@
                     dec_grad_ref[target, :, columns] = part
                 else:
                     dec_grad_ref[target, :, columns] += part
+            if c == chunks - 1:
+                copy = pltpu.make_async_copy(dec_grad_ref.at[target], dec_grad_hbm.at[target], out_sem.at[target])
+                copy.start()
+                stored.append(copy)
 
     def finish(c):
         arrive(("back", c))
         total = back_part[c, width] + (back_recv[c, 0] + back_recv[c, 1] + back_recv[c, 2])
-        pre_grad_ref[c * rows : (c + 1) * rows, :] = total * slope[c]
+        pre_grad_ref[c] = total * slope[c]
+        copy = pltpu.make_async_copy(
+            pre_grad_ref.at[c], pre_grad_hbm.at[c * rows : (c + 1) * rows], out_sem.at[2 + c]
+        )
+        copy.start()
+        stored.append(copy)
 
     run = locals()
     stages = {name: run[name] for name, _ in STAGES}
@@ -398,6 +411,33 @@
         stages[name](c)
     for copy in sent:
         copy.wait_send()
+    for copy in stored:
+        copy.wait()
+
+
+def settle(*refs):
+    count = len(refs) // 3
+    sources, results, held = refs[:count], refs[count : 2 * count], refs[2 * count : 3 * count]
+    in_sem, out_sem = refs[3 * count :]
+    pieces = []
+    for source, result, hold in zip(sources, results, held):
+        step = 64
+        for start in range(0, source.shape[0], step):
+            at = slice(start, start + step)
+            n = len(pieces)
+            pieces.append(
+                (
+                    pltpu.make_async_copy(source.at[at], hold.at[at], in_sem.at[n]),
+                    pltpu.make_async_copy(hold.at[at], result.at[at], out_sem.at[n]),
+                )
+            )
+    for load, _ in pieces:
+        load.start()
+    for load, store in pieces:
+        load.wait()
+        store.start()
+    for _, store in pieces:
+        store.wait()
 
 
 def local(inputs, targets, w_enc, b_enc, thresholds, w_dec, b_dec):
@@ -406,7 +446,6 @@
     c = CHUNKS
     rows = tokens // (NX * c)
     half = width // 2
-    vmem = pl.BlockSpec(memory_space=pltpu.VMEM)
     hbm = pl.BlockSpec(memory_space=pltpu.HBM)
     dma = pltpu.SemaphoreType.DMA
     dec_grad, pre_grad = pl.pallas_call(
@@ -416,8 +455,11 @@
             jax.ShapeDtypeStruct((tokens // NX, feats), F32),
         ),
         in_specs=[hbm] * 7,
-        out_specs=(vmem, vmem),
+        out_specs=(hbm, hbm),
         scratch_shapes=[
+            pltpu.VMEM(w_dec.shape[1:], F32),
+            pltpu.VMEM((c, rows, feats), F32),
+            dma((2 + c,)),
             pltpu.VMEM(targets.shape, F32),
             pltpu.VMEM((1, feats), F32),
             pltpu.VMEM((1, feats), F32),
@@ -466,7 +508,16 @@
         w_dec[0],
         b_dec,
     )
-    return dec_grad[None], pre_grad[None]
+    parts = (dec_grad.reshape(2 * feats, width), pre_grad)
+    count = sum(part.shape[0] for part in parts) // 64
+    dec_grad, pre_grad = pl.pallas_call(
+        settle,
+        out_shape=tuple(jax.ShapeDtypeStruct(part.shape, F32) for part in parts),
+        in_specs=[hbm] * 2,
+        out_specs=(hbm,) * 2,
+        scratch_shapes=[pltpu.VMEM(part.shape, F32) for part in parts] + [dma((count,)), dma((count,))],
+    )(*parts)
+    return dec_grad.reshape(w_dec.shape), pre_grad[None]
 
 
 def solution(mesh):

time: 104 us -> 99.6 us (0.958)
  local copies, waits for them, and re-layouts: 3.01 us -> 0 us
  Pallas kernels: 100 us -> 98.6 us
    pallas_call x1, Pallas kernels: 100 us -> 96.4 us  [local(): pl.pallas_call(kernel, out_shape=(jax.ShapeDtypeStruct(w_dec.shape[1:], F...]
    unnamed x4 -> x0, local copies, waits for them, and re-layouts: 3.01 us -> none
    pallas_call x0 -> x1, Pallas kernels: none -> 2.24 us  [local(): pl.pallas_call(settle, out_shape=tuple((jax.ShapeDtypeStruct(part.shape,...]
where the time goes in v3:
time: 99.6 us; the launch traced here: 99.4 us
  Pallas kernels  98.6 us (99%)
    pallas_call x1, Pallas kernels, local(): pl.pallas_call(kernel, out_shape=(jax.ShapeDtypeStruct(w_dec.shape[1:], F...  96.4 us
    pallas_call x1, Pallas kernels, local(): pl.pallas_call(settle, out_shape=tuple((jax.ShapeDtypeStruct(part.shape,...  2.24 us

profile of v3, /device:TPU:1, one launch (start us, length us, event | category | flops | bytes accessed | tf_op | source)
XLA Modules:
  0.0 99.4 jit_solution(4191883444455359569)
XLA Ops:
  0.6 96.4 %shard_map.86 = (f32[2,256,512]{2,1,0:T(8,128)}, f32[256,256]{1,0:T(8,128)}) custom-call(f32[4,8,32,512]{3,2,1,0:T(8,128)} %bitcast.6, f32[2,8,512]{2,1,0:T(8,128)} %targets_hbm.1, f32[512,256]{1,0:T(8,128)} %bitcast.9, f32[1,256]{1,0:T(1,128)} %b_enc_hbm.1, f32[1,256]{1,0:T(1,128)} %thr_hbm.1, f32[2,256,512]{2,1,0:T(8,128)} %bitcast.8, f32[2,512]{1,0:T(2,128)} %b_dec_hbm.1), custom_call_target="tpu_custom_call" | custom-call | tf_op jit(solution)/shard_map/pallas_call | solution.py:451
  97.0 2.2 %shard_map.87 = (f32[512,512]{1,0:T(8,128)}, f32[256,256]{1,0:T(8,128)}) custom-call(f32[512,512]{1,0:T(8,128)} %bitcast.7, f32[256,256]{1,0:T(8,128)} %get-tuple-element.7.refs_1_), custom_call_target="tpu_custom_call" | custom-call | tf_op jit(solution)/shard_map/pallas_call | solution.py:513

commit v4 on v3

--- a/solution.py
+++ b/solution.py
@@ -21,14 +21,14 @@
     ("pre", 1.5),
     ("gate", 6.0),
     ("recon", 6.0),
-    ("core_sum", 1.8),
+    ("core_sum", 2.8),
     ("y_sum", 5.3),
     ("zlo_sum", 5.1),
     ("zhi_sum", 7.5),
     ("zhi_all", 7.5),
     ("zlo_all", 5.1),
     ("y_all", 5.3),
-    ("back", 1.8),
+    ("back", 2.8),
     ("grad", 0.3),
     ("finish", 6.0),
 )
@@ -390,12 +390,12 @@
                     dec_grad_ref[target, :, columns] = part
                 else:
                     dec_grad_ref[target, :, columns] += part
-            if c == chunks - 1:
+    def finish(c):
+        if c == chunks - 1:
+            for target in range(2):
                 copy = pltpu.make_async_copy(dec_grad_ref.at[target], dec_grad_hbm.at[target], out_sem.at[target])
                 copy.start()
                 stored.append(copy)
-
-    def finish(c):
         arrive(("back", c))
         total = back_part[c, width] + (back_recv[c, 0] + back_recv[c, 1] + back_recv[c, 2])
         pre_grad_ref[c] = total * slope[c]

time: 99.6 us -> 99.2 us (level)
  no operation moved by 1% of the time
where the time goes in v4:
time: 99.2 us; the launch traced here: 99 us
  Pallas kernels  98.2 us (99%)
    pallas_call x1, Pallas kernels, local(): pl.pallas_call(kernel, out_shape=(jax.ShapeDtypeStruct(w_dec.shape[1:], F...  96 us
    pallas_call x1, Pallas kernels, local(): pl.pallas_call(settle, out_shape=tuple((jax.ShapeDtypeStruct(part.shape,...  2.24 us

profile of v4, /device:TPU:1, one launch (start us, length us, event | category | flops | bytes accessed | tf_op | source)
XLA Modules:
  0.0 99.0 jit_solution(10100345231787687391)
XLA Ops:
  0.6 96.0 %shard_map.86 = (f32[2,256,512]{2,1,0:T(8,128)}, f32[256,256]{1,0:T(8,128)}) custom-call(f32[4,8,32,512]{3,2,1,0:T(8,128)} %bitcast.6, f32[2,8,512]{2,1,0:T(8,128)} %targets_hbm.1, f32[512,256]{1,0:T(8,128)} %bitcast.9, f32[1,256]{1,0:T(1,128)} %b_enc_hbm.1, f32[1,256]{1,0:T(1,128)} %thr_hbm.1, f32[2,256,512]{2,1,0:T(8,128)} %bitcast.8, f32[2,512]{1,0:T(2,128)} %b_dec_hbm.1), custom_call_target="tpu_custom_call" | custom-call | tf_op jit(solution)/shard_map/pallas_call | solution.py:451
  96.6 2.2 %shard_map.87 = (f32[512,512]{1,0:T(8,128)}, f32[256,256]{1,0:T(8,128)}) custom-call(f32[512,512]{1,0:T(8,128)} %bitcast.7, f32[256,256]{1,0:T(8,128)} %get-tuple-element.7.refs_1_), custom_call_target="tpu_custom_call" | custom-call | tf_op jit(solution)/shard_map/pallas_call | solution.py:513
